TPU v7x, 128 devices: a whole 4x4x4 slice. The times are simulated.
128 devices in a mesh: row: 8 (over y_lo, x), col: 16 (over y_hi, z, core).
Axes of the slice: x: 4, y: 4 (y_hi: 2, y_lo: 2; y = y_hi * 2 + y_lo), z: 4, core: 2. Of those that a mesh axis runs over, the one named last changes fastest.
Arguments:
- sign_iterate: bfloat16 [8192, 8192], P('row', 'col'), may hold values from -6 to 6
- sign_square: bfloat16 [8192, 8192], P('row', 'col'), may hold values from -0.125 to 0.125
- pattern_x: int32 [64, 64], P('row', 'col'), may hold values 0 or 1
- pattern_y: int32 [64, 64], P('row', 'col'), may hold values 0 or 1
- pattern_product: int32 [64, 64], P('row', 'col'), may hold values 0 or 1
- orbital_energy: bfloat16 [8192], P('row'), may hold values from -3 to 1
- pair_dest: int32 [128, 128, 1], P(('row', 'col')), may hold values from 0 to 127; in each aligned block of 128 rows (0 to 127, 128 to 255, ..., all dimensions but the last counted through in order) at most 2 rows name the same one
- pair_block: int32 [128, 128], P(('row', 'col')), may hold values from 0 to 31
- force_h: bfloat16 [32768, 128, 128], P(('row', 'col')), may hold values from -0.5 to 0.5
- force_s: bfloat16 [32768, 128, 128], P(('row', 'col')), may hold values from -0.5 to 0.5
Outputs:
- sign_next: bfloat16 [8192, 8192], P('row', 'col')
- forces: float32 [32768], P(('row', 'col'))
Inputs may be any that keep to these rules, and one draw needn't show every extreme that they name: `pair_dest`: among the 128 entries of one device no owner is named more than 2 times, a bound that some block reaches. `pair_block`: A row-major index into the device's own 8 x 4 grid of blocks.
All inputs are finite; a program needn't handle non-finite values. No bound on the sum of `pattern_x` or of `pattern_y` or of `pattern_product` on one device may be relied on, other than what follows from the above.
Results may differ from a plain program's by a relative error of at most 0.003.
Values may be sent and summed in bfloat16 or wider, within the bound.
No kernel may reach another device: no remote copies, remote signals or barrier semaphores. Data moves between devices by JAX's collectives and lax.ppermute only.
A program may use at most 128 MiB of HBM per device.

v0:
```python
import jax
import jax.numpy as jnp
from jax import lax
from jax.sharding import PartitionSpec as P

BS = 128
QB = 4
CAP = 2


def masked_tile(tile, pattern):
    rows, cols = tile.shape
    shaped = tile.reshape(rows // BS, BS, cols // BS, BS) * pattern[:, None, :, None].astype(
        tile.dtype
    )
    return shaped.reshape(rows, cols)


def tile_blocks(tile):
    rows, cols = tile.shape
    shaped = tile.reshape(rows // BS, BS, cols // BS, BS).transpose(0, 2, 1, 3)
    return shaped.reshape(rows // BS * (cols // BS), BS * BS)


def rank_within(dest):
    entries = dest.shape[-1]
    order = jnp.arange(entries, dtype=jnp.int32)
    same = (dest[..., :, None] == dest[..., None, :]) & (order[None, :] < order[:, None])
    return jnp.sum(same.astype(jnp.int32), axis=-1)


def shards(
    sign_iterate,
    sign_square,
    pattern_x,
    pattern_y,
    pattern_product,
    orbital_energy,
    pair_dest,
    pair_block,
    force_h,
    force_s,
):
    rows_x, cols_x = sign_iterate.shape
    xmask = masked_tile(sign_iterate, pattern_x)
    ymask = masked_tile(sign_square, pattern_y)
    y_whole = lax.all_gather(ymask, "row", axis=0, tiled=True)
    product = jnp.dot(
        lax.all_gather(xmask, "col", axis=1, tiled=True),
        y_whole,
        preferred_element_type=jnp.float32,
    )
    product = masked_tile(product, pattern_product)
    xnew = 1.5 * xmask.astype(jnp.float32) - 0.5 * product
    sign_next = xnew.astype(jnp.bfloat16)
    global_rows = lax.axis_index("row") * rows_x + jnp.arange(rows_x, dtype=jnp.int32)
    global_cols = lax.axis_index("col") * cols_x + jnp.arange(cols_x, dtype=jnp.int32)
    identity = (global_rows[:, None] == global_cols[None, :]).astype(jnp.float32)
    density = (0.5 * identity - 0.5 * xnew).astype(jnp.bfloat16)
    dens_blocks = tile_blocks(density)
    n_rows = lax.axis_size("row")
    n_cols = lax.axis_size("col")
    devices = n_rows * n_cols
    slots = devices * CAP
    local_rows = rows_x // BS
    dest = pair_dest[0, :, 0]
    wanted = pair_block[0]
    rank = rank_within(dest)
    slot = dest * CAP + rank
    pick_slot = (jnp.arange(slots, dtype=jnp.int32)[:, None] == slot[None, :]).astype(jnp.bfloat16)
    pick_block = (
        wanted[:, None] == jnp.arange(dens_blocks.shape[0], dtype=jnp.int32)[None, :]
    ).astype(jnp.bfloat16)
    routing_table = jnp.dot(pick_slot, pick_block, preferred_element_type=jnp.float32).astype(
        jnp.bfloat16
    )
    send_dens = jnp.dot(routing_table, dens_blocks, preferred_element_type=jnp.float32).astype(
        jnp.bfloat16
    )
    pick_row = ((wanted // QB)[:, None] == jnp.arange(local_rows, dtype=jnp.int32)[None, :]).astype(
        jnp.bfloat16
    )
    slot_rows = jnp.dot(pick_slot, pick_row, preferred_element_type=jnp.float32).astype(
        jnp.bfloat16
    )
    send_energy = jnp.dot(
        slot_rows, orbital_energy.reshape(local_rows, BS), preferred_element_type=jnp.float32
    ).astype(jnp.bfloat16)
    payload = jnp.concatenate([send_dens.reshape(slots, BS, BS), send_energy[:, None, :]], axis=1)
    height = BS + 1
    received = lax.all_to_all(
        payload.reshape(devices, CAP, height * BS),
        ("row", "col"),
        split_axis=0,
        concat_axis=0,
        tiled=True,
    )
    received = received.reshape(slots, height, BS)
    recv_dens = received[:, :BS, :]
    energies = received[:, BS, :].astype(jnp.float32)
    h_term = jnp.einsum("sab,sab->s", recv_dens, force_h, preferred_element_type=jnp.float32)
    s_rows = jnp.einsum("sab,sab->sa", recv_dens, force_s, preferred_element_type=jnp.float32)
    forces = h_term - jnp.sum(energies * s_rows, axis=1)
    return (sign_next, forces)


def solution(mesh):
    in_specs = (
        P("row", "col"),
        P("row", "col"),
        P("row", "col"),
        P("row", "col"),
        P("row", "col"),
        P("row"),
        P(("row", "col"), None, None),
        P(("row", "col"), None),
        P(("row", "col"), None, None),
        P(("row", "col"), None, None),
    )
    out_specs = (P("row", "col"), P(("row", "col")))
    return jax.shard_map(shards, mesh=mesh, in_specs=in_specs, out_specs=out_specs, check_vma=False)
```

profile of v0, /device:TPU:6, one launch (start us, length us, event | category | flops | bytes accessed | tf_op | source)
XLA Modules:
  0.0 425.4 jit_solution(5564351684399702492)
XLA Ops:
  7.2 0.0 all-gather.5.cloned.1.call-start
  7.3 0.7 convert_element_type.48
  7.9 0.1 copy.22
  8.0 0.3 mul.72
  8.4 2.4 bitcast_multiply_fusion.1
  10.8 0.0 all-gather.5.cloned.1.call-update
  10.8 0.0 all-gather.3.cloned.1.call-start
  10.9 0.7 convert_element_type.46
  11.6 0.1 copy.21
  11.7 0.3 mul.67
  12.0 2.3 bitcast_multiply_fusion.2
  14.3 0.0 all-gather.3.cloned.1.call-update
  14.4 0.1 copy.23
  14.5 0.2 convert_reduce_fusion
  14.7 0.5 fusion.5
  15.2 0.1 copy.25
  15.3 87.7 %all-gather.5.cloned.1.call-done = bf16[8192,512]{1,0:T(8,128)(2,1)} async-done(((bf16[1024,512]{1,0:T(8,128)(2,1)}), bf16[8192,512]{1,0:T(8,128)(2,1)}) %all-gather.5.cloned.1.call-update) | async-done | bytes 8388624 | tf_op jit(solution)/shard_map/all_gather | solution.py:47
  103.0 123.0 %all-gather.3.cloned.1.call-done = bf16[1024,8192]{1,0:T(8,128)(2,1)} async-done(((bf16[1024,512]{1,0:T(8,128)(2,1)}), bf16[1024,8192]{1,0:T(8,128)(2,1)}) %all-gather.3.cloned.1.call-update) | async-done | bytes 16777232 | tf_op jit(solution)/shard_map/all_gather | solution.py:49
  226.0 0.3 mul.75
  226.3 16.1 %subtract_convert_fusion = (bf16[1024,512]{1,0:T(8,128)(2,1)S(1)}, bf16[1024,512]{1,0:T(8,128)(2,1)}) fusion(s32[512]{0:T(512)S(1)} %iota_add_fusion.1, s32[1024]{0:T(1024)S(1)} %iota_add_fusion, f32[128,8,4,128]{3,2,1,0:T(4,128)S(1)} %bitcast.41, bf16[1024,8192]{1,0:T(8,128)(2,1)} %all-gather.3.cloned.1.call-done, ...), kind=kOutput, calls=%fused_computation.10 | convolution fusion | flops 8595701760 | bytes 30414848 | tf_op jit(solution)/shard_map/dot_general | solution.py:48
  242.4 0.3 reshape.86
  242.7 0.2 copy.24
  243.0 5.2 %fusion.2 = bf16[32,8,128,128]{3,1,2,0:T(8,128)(2,1)} fusion(bf16[4,8,128,128]{3,2,1,0:T(8,128)(2,1)S(1)} %bitcast.38, s32[128]{0:T(128)S(1)} %get-tuple-element.8, s32[128]{0:T(128)S(1)} %bitcast.43), kind=kOutput, calls=%fused_computation.6 | convolution fusion | flops 274771968 | bytes 9438208 | tf_op jit(solution)/shard_map/dot_general | solution.py:77
  248.2 9.2 %copy.40 = bf16[32,8,128,128]{3,2,1,0:T(8,128)(2,1)} copy(bf16[32,8,128,128]{3,1,2,0:T(8,128)(2,1)} %fusion.2) | data formatting | bytes 16777216
  257.4 9.0 %pad_maximum_fusion = bf16[256,129,128]{2,1,0:T(8,128)(2,1)} fusion(bf16[256,1,128]{2,1,0:T(2,128)(2,1)S(1)} %copy.25, bf16[256,128,128]{2,1,0:T(8,128)(2,1)} %bitcast.37), kind=kLoop, calls=%fused_computation.5 | loop fusion | flops 16908288 | bytes 16908288 | tf_op jit(solution)/shard_map/concatenate | solution.py:89
  266.4 13.2 %reshape.90 = bf16[128,2,16512]{2,1,0:T(2,128)(2,1)} reshape(bf16[256,129,128]{2,1,0:T(8,128)(2,1)} %pad_maximum_fusion) | data formatting | bytes 16908288 | tf_op jit(solution)/shard_map/reshape | solution.py:92
  279.6 111.1 %all_to_all.5 = bf16[128,2,16512]{2,1,0:T(2,128)(2,1)} all-to-all(bf16[128,2,16512]{2,1,0:T(2,128)(2,1)} %reshape.90), channel_id=1, replica_groups=mesh['row'=8,'col'=16] {'row','col'}, dimensions={0} | all-to-all | bytes 16908288 | tf_op jit(solution)/shard_map/all_to_all | solution.py:91
  390.7 14.2 %reshape.91 = bf16[256,129,128]{2,1,0:T(8,128)(2,1)} reshape(bf16[128,2,16512]{2,1,0:T(2,128)(2,1)} %all_to_all.5) | data formatting | bytes 16908288 | tf_op jit(solution)/shard_map/reshape | solution.py:98
  404.9 1.1 slice_convert_fusion
  406.0 11.8 %fusion.1 = (f32[256,128]{1,0:T(8,128)S(1)}, f32[256]{0:T(256)S(1)}) fusion(bf16[256,128,128]{2,1,0:T(8,128)(2,1)} %param.19, bf16[256,129,128]{2,1,0:T(8,128)(2,1)} %reshape.91, bf16[256,128,128]{2,1,0:T(8,128)(2,1)} %param.18), kind=kLoop, calls=%fused_computation.4 | loop fusion | flops 29327104 | bytes 25297920 | tf_op jit(solution)/shard_map/sab,sab->sa/dot_general | solution.py:102
  417.8 0.1 multiply_reduce_fusion
  417.9 0.6 sub.18
  (14 shorter events, 0.0 us)
Async XLA Ops:
  7.2 7.5 %copy-start = (bf16[1024]{0:T(1024)(128)(2,1)S(1)}, bf16[1024]{0:T(1024)(128)(2,1)}, u32[]{:S(2)}) copy-start(bf16[1024]{0:T(1024)(128)(2,1)} %param.15) | copy-start | bytes 6148
  7.2 7.2 %copy-start.3 = (s32[8,4]{0,1:T(4,128)S(1)}, s32[8,4]{0,1:T(4,128)}, u32[]{:S(2)}) copy-start(s32[8,4]{0,1:T(4,128)} %param.14) | copy-start | bytes 388
  7.2 7.3 %copy-start.4 = (s32[1,128,1]{1,2,0:T(1,128)S(1)}, s32[1,128,1]{1,2,0:T(1,128)}, u32[]{:S(2)}) copy-start(s32[1,128,1]{1,2,0:T(1,128)} %param.16) | copy-start | bytes 1540
  7.2 7.5 %copy-start.2 = (s32[1,128]{1,0:T(1,128)S(1)}, s32[1,128]{1,0:T(1,128)}, u32[]{:S(2)}) copy-start(s32[1,128]{1,0:T(1,128)} %param.17) | copy-start | bytes 1540
  7.2 95.8 %all-gather.5.cloned.1.call-start = ((), (), s32[]{:S(2)}) async-start(), calls=%async_computation.2 | async-start | bytes 9437184 | tf_op jit(solution)/shard_map/all_gather | solution.py:47
  10.8 215.1 %all-gather.3.cloned.1.call-start = ((), (), s32[]{:S(2)}) async-start(), calls=%async_computation.1 | async-start | bytes 17825792 | tf_op jit(solution)/shard_map/all_gather | solution.py:49
  404.9 13.7 %copy-start.1 = (bf16[1024]{0:T(1024)(128)(2,1)S(1)}, bf16[1024]{0:T(1024)(128)(2,1)}, u32[]{:S(2)}) copy-start(bf16[1024]{0:T(1024)(128)(2,1)} %param.15) | copy-start | bytes 6148
Sparse Core Ops, SparseCore 0:
  11.0 92.0 all-gather.4
  105.8 120.0 all-gather.2
where the time goes:
time: 426 us; the launch traced here: 425 us
  waiting for transfers between devices  211 us (50%)
  blocking collectives  111 us (26%)
  local copies, waits for them, and re-layouts  38.6 us (9%)
  other arithmetic  28.9 us (7%)
  matrix products  21.8 us (5%)
  between operations  14.2 us (3%)
    all_gather x1, waiting for transfers between devices, shards(): lax.all_gather(xmask, 'col', axis=1, tiled=True)  123 us
    all_to_all x1, blocking collectives, shards(): lax.all_to_all(payload.reshape(devices, CAP, height * BS), ('row', 'col')...  111 us
    all_gather x1, waiting for transfers between devices, shards(): y_whole = lax.all_gather(ymask, 'row', axis=0, tiled=True)  87.7 us
    dot_general x1, matrix products, shards(): jnp.dot(lax.all_gather(xmask, 'col', axis=1, tiled=True), y_whole, prefer...  16.1 us
    reshape x1, local copies, waits for them, and re-layouts, shards(): received = received.reshape(slots, height, BS)  14.2 us
    reshape x1, local copies, waits for them, and re-layouts, shards(): payload.reshape(devices, CAP, height * BS)  13.2 us
    dot_general x1, other arithmetic, shards(): jnp.einsum('sab,sab->sa', recv_dens, force_s, preferred_element_type=jnp....  11.8 us
    unnamed x11, local copies, waits for them, and re-layouts  9.24 us
  transfers between devices with their start and end apart: 2, of which 2 were waited for; matrix products, arithmetic and copies ran while one was open for 1% of the time, Pallas kernels for 0%

commit v1 on v0

--- a/solution.py
+++ b/solution.py
@@ -46,7 +46,9 @@
     ymask = masked_tile(sign_square, pattern_y)
     y_whole = lax.all_gather(ymask, "row", axis=0, tiled=True)
     product = jnp.dot(
-        lax.all_gather(xmask, "col", axis=1, tiled=True),
+        jnp.concatenate(
+            lax.all_to_all(jnp.stack([xmask] * lax.axis_size("col")), "col", 0, 0), axis=1
+        ),
         y_whole,
         preferred_element_type=jnp.float32,
     )

time: 426 us -> 626 us (1.47)
  the two profiles are of different devices: /device:TPU:6 before, /device:TPU:23 now
where the time goes in v1:
time: 626 us; the launch traced here: 624 us
  waiting for transfers between devices  428 us (68%)
  local copies, waits for them, and re-layouts  106 us (17%)
  starting transfers between devices  29.5 us (5%)
  other arithmetic  26.4 us (4%)
  matrix products  20.2 us (3%)
  between operations  14.3 us (2%)
    all_to_all x1, waiting for transfers between devices, shards(): lax.all_to_all(jnp.stack([xmask] * lax.axis_size('col')), 'col', 0, 0)  220 us
    all_to_all x1, waiting for transfers between devices, shards(): lax.all_to_all(payload.reshape(devices, CAP, height * BS), ('row', 'col')...  117 us
    all_gather x1, waiting for transfers between devices, shards(): y_whole = lax.all_gather(ymask, 'row', axis=0, tiled=True)  90.7 us
    dot_general x2, local copies, waits for them, and re-layouts, shards(): jnp.dot(jnp.concatenate(lax.all_to_all(jnp.stack([xmask] * lax.axis_size(...  37.6 us
    all_to_all x1, starting transfers between devices, shards(): lax.all_to_all(payload.reshape(devices, CAP, height * BS), ('row', 'col')...  20.7 us
    reshape x1, local copies, waits for them, and re-layouts, shards(): jnp.concatenate(lax.all_to_all(jnp.stack([xmask] * lax.axis_size('col')),...  18.4 us
    dot_general x1, matrix products, shards(): jnp.dot(jnp.concatenate(lax.all_to_all(jnp.stack([xmask] * lax.axis_size(...  14.5 us
    reshape x1, local copies, waits for them, and re-layouts, shards(): received = received.reshape(slots, height, BS)  14.2 us
  transfers between devices with their start and end apart: 3, of which 3 were waited for; matrix products, arithmetic and copies ran while one was open for 3% of the time, Pallas kernels for 0%

profile of v1, /device:TPU:23, one launch (start us, length us, event | category | flops | bytes accessed | tf_op | source)
XLA Modules:
  0.0 623.9 jit_solution(11308408525288781365)
XLA Ops:
  7.2 0.7 convert_element_type.46
  7.9 1.5 copy.36
  9.4 0.2 mul.69
  9.6 0.1 bitcast_multiply_fusion.1
  9.7 0.5 copy.37
  10.3 6.0 stack.3
  16.3 8.8 %all-to-all-start = ((bf16[16,1024,512]{2,1,0:T(8,128)(2,1)}), bf16[16,1024,512]{2,1,0:T(8,128)(2,1)}, u32[]{:S(2)}, u32[]{:S(2)}) async-start(bf16[16,1024,512]{2,1,0:T(8,128)(2,1)} %stack.3), calls=%async_computation | async-start | bytes 33554432 | tf_op jit(solution)/shard_map/all_to_all | solution.py:50
  25.2 0.3 mul.74
  25.5 1.1 bitcast_multiply_fusion
  26.8 0.2 convert_reduce_fusion
  27.0 0.5 fusion.8
  27.6 90.7 %all-gather.2.cloned.1.call-done = bf16[8192,512]{1,0:T(8,128)(2,1)} async-done(((bf16[1024,512]{1,0:T(8,128)(2,1)}), bf16[8192,512]{1,0:T(8,128)(2,1)}) %all-gather.2.cloned.1.call-update) | async-done | bytes 8388624 | tf_op jit(solution)/shard_map/all_gather | solution.py:47
  118.3 12.0 %copy.40 = bf16[512,8192]{1,0:T(8,128)(2,1)} copy(bf16[512,8192]{0,1:T(8,128)(2,1)} %bitcast.59) | data formatting | bytes 16777216 | tf_op jit(solution)/shard_map/dot_general | solution.py:48
  130.3 220.1 %all-to-all-done = bf16[16,1024,512]{2,1,0:T(8,128)(2,1)} async-done(((bf16[16,1024,512]{2,1,0:T(8,128)(2,1)}), bf16[16,1024,512]{2,1,0:T(8,128)(2,1)}, u32[]{:S(2)}, u32[]{:S(2)}) %all-to-all-start) | async-done | bytes 16777248 | tf_op jit(solution)/shard_map/all_to_all | solution.py:50
  350.4 18.4 %copy.38 = bf16[1024,16,512]{2,1,0:T(8,128)(2,1)} copy(bf16[1024,16,512]{2,0,1:T(8,128)(2,1)} %bitcast) | data formatting | bytes 33554432 | tf_op jit(solution)/shard_map/reshape | solution.py:49
  368.9 25.6 %reshape.106 = bf16[8,128,8192,1]{2,1,0,3:T(8,128)(2,1)} reshape(bf16[1024,16,512]{2,1,0:T(8,128)(2,1)} %copy.38) | data formatting | bytes 33554432 | tf_op jit(solution)/shard_map/dot_general | solution.py:48
  394.5 14.5 %multiply_multiply_fusion = f32[8,128,4,128]{3,1,2,0:T(8,128)} fusion(bf16[4,128,8192,1]{2,1,0,3:T(8,128)(2,1)} %bitcast.60, bf16[8,128,8192,1]{2,1,0,3:T(8,128)(2,1)} %reshape.106, f32[8,4]{1,0:T(8,128)S(1)} %copy.41), kind=kOutput, calls=%fused_computation.11 | convolution fusion | flops 8590983168 | bytes 27263104 | tf_op jit(solution)/shard_map/dot_general | solution.py:48
  409.0 2.0 copy.42
  411.1 1.6 fusion.9
  412.7 0.3 copy.60
  413.0 0.8 copy.43
  413.8 5.2 fusion.4
  419.0 9.2 %copy.62 = bf16[32,8,128,128]{3,2,1,0:T(8,128)(2,1)} copy(bf16[32,8,128,128]{3,1,2,0:T(8,128)(2,1)} %fusion.4) | data formatting | bytes 16777216
  428.2 9.0 %pad_maximum_fusion = bf16[256,129,128]{2,1,0:T(8,128)(2,1)} fusion(bf16[256,1,128]{2,1,0:T(2,128)(2,1)S(1)} %copy.44, bf16[256,128,128]{2,1,0:T(8,128)(2,1)} %bitcast.58), kind=kLoop, calls=%fused_computation.7 | loop fusion | flops 16908288 | bytes 16908288 | tf_op jit(solution)/shard_map/concatenate | solution.py:91
  437.2 13.2 %reshape.103 = bf16[128,2,16512]{2,1,0:T(2,128)(2,1)} reshape(bf16[256,129,128]{2,1,0:T(8,128)(2,1)} %pad_maximum_fusion) | data formatting | bytes 16908288 | tf_op jit(solution)/shard_map/reshape | solution.py:94
  450.4 20.7 %all-to-all-start.1 = ((bf16[128,2,16512]{2,1,0:T(2,128)(2,1)}), bf16[128,2,16512]{2,1,0:T(2,128)(2,1)}, u32[]{:S(2)}, u32[]{:S(2)}) async-start(bf16[128,2,16512]{2,1,0:T(2,128)(2,1)} %reshape.103), calls=%async_computation.1 | async-start | bytes 16908288 | tf_op jit(solution)/shard_map/all_to_all | solution.py:93
  471.1 1.3 copy.45
  472.4 116.7 %all-to-all-done.1 = bf16[128,2,16512]{2,1,0:T(2,128)(2,1)} async-done(((bf16[128,2,16512]{2,1,0:T(2,128)(2,1)}), bf16[128,2,16512]{2,1,0:T(2,128)(2,1)}, u32[]{:S(2)}, u32[]{:S(2)}) %all-to-all-start.1) | async-done | bytes 8454176 | tf_op jit(solution)/shard_map/all_to_all | solution.py:93
  589.2 14.2 %reshape.104 = bf16[256,129,128]{2,1,0:T(8,128)(2,1)} reshape(bf16[128,2,16512]{2,1,0:T(2,128)(2,1)} %all-to-all-done.1) | data formatting | bytes 16908288 | tf_op jit(solution)/shard_map/reshape | solution.py:100
  603.4 1.1 slice_convert_fusion
  604.5 11.8 %fusion.1 = (f32[256,128]{1,0:T(8,128)S(1)}, f32[256]{0:T(256)S(1)}) fusion(bf16[256,128,128]{2,1,0:T(8,128)(2,1)} %param.19, bf16[256,129,128]{2,1,0:T(8,128)(2,1)} %reshape.104, bf16[256,128,128]{2,1,0:T(8,128)(2,1)} %param.18), kind=kLoop, calls=%fused_computation.4 | loop fusion | flops 29327104 | bytes 25297920 | tf_op jit(solution)/shard_map/sab,sab->sa/dot_general | solution.py:104
  616.5 0.6 sub.18
  (27 shorter events, 0.5 us)
Async XLA Ops:
  7.2 19.8 %copy-start = (bf16[1024]{0:T(1024)(128)(2,1)S(1)}, bf16[1024]{0:T(1024)(128)(2,1)}, u32[]{:S(2)}) copy-start(bf16[1024]{0:T(1024)(128)(2,1)} %param.15) | copy-start | bytes 6148
  16.2 8.8 %copy-start.5 = (s32[8,4]{0,1:T(4,128)S(1)}, s32[8,4]{0,1:T(4,128)}, u32[]{:S(2)}) copy-start(s32[8,4]{0,1:T(4,128)} %param.13) | copy-start | bytes 388
  16.2 9.3 %copy-start.3 = (bf16[1024,512]{1,0:T(8,128)(2,1)S(1)}, bf16[1024,512]{1,0:T(8,128)(2,1)}, u32[]{:S(2)}) copy-start(bf16[1024,512]{1,0:T(8,128)(2,1)} %param.11) | copy-start | bytes 3145732
  16.2 10.5 %copy-start.6 = (s32[8,4]{0,1:T(4,128)S(1)}, s32[8,4]{0,1:T(4,128)}, u32[]{:S(2)}) copy-start(s32[8,4]{0,1:T(4,128)} %param.14) | copy-start | bytes 388
  16.2 10.6 %copy-start.7 = (s32[1,128,1]{1,2,0:T(1,128)S(1)}, s32[1,128,1]{1,2,0:T(1,128)}, u32[]{:S(2)}) copy-start(s32[1,128,1]{1,2,0:T(1,128)} %param.16) | copy-start | bytes 1540
  16.2 10.7 %copy-start.4 = (s32[1,128]{1,0:T(1,128)S(1)}, s32[1,128]{1,0:T(1,128)}, u32[]{:S(2)}) copy-start(s32[1,128]{1,0:T(1,128)} %param.17) | copy-start | bytes 1540
  16.3 334.2 %all-to-all-start = ((bf16[16,1024,512]{2,1,0:T(8,128)(2,1)}), bf16[16,1024,512]{2,1,0:T(8,128)(2,1)}, u32[]{:S(2)}, u32[]{:S(2)}) async-start(bf16[16,1024,512]{2,1,0:T(8,128)(2,1)} %stack.3), calls=%async_computation | async-start | bytes 33554432 | tf_op jit(solution)/shard_map/all_to_all | solution.py:50
  25.0 93.3 %all-gather.2.cloned.1.call-start = ((), (), s32[]{:S(2)}) async-start(), calls=%async_computation.2 | async-start | bytes 9437184 | tf_op jit(solution)/shard_map/all_gather | solution.py:47
  450.4 20.7 %copy-start.2 = (bf16[1024,512]{0,1:T(8,128)(2,1)S(1)}, bf16[1024,512]{0,1:T(8,128)(2,1)}, u32[]{:S(2)}) copy-start(bf16[1024,512]{0,1:T(8,128)(2,1)} %get-tuple-element.11) | copy-start | bytes 3145732
  450.4 138.8 %all-to-all-start.1 = ((bf16[128,2,16512]{2,1,0:T(2,128)(2,1)}), bf16[128,2,16512]{2,1,0:T(2,128)(2,1)}, u32[]{:S(2)}, u32[]{:S(2)}) async-start(bf16[128,2,16512]{2,1,0:T(2,128)(2,1)} %reshape.103), calls=%async_computation.1 | async-start | bytes 16908288 | tf_op jit(solution)/shard_map/all_to_all | solution.py:93
  603.4 13.7 %copy-start.1 = (bf16[1024]{0:T(1024)(128)(2,1)S(1)}, bf16[1024]{0:T(1024)(128)(2,1)}, u32[]{:S(2)}) copy-start(bf16[1024]{0:T(1024)(128)(2,1)} %param.15) | copy-start | bytes 6148
Sparse Core Ops, SparseCore 0:
  28.1 90.1 all-gather.1
